TPU v7x, 32 devices: a whole 2x2x4 slice. The times are simulated.
32 devices in a mesh: seq: 4 (over y, x), batch: 8 (over z, core).
Axes of the slice: x: 2, y: 2, z: 4, core: 2. Of those that a mesh axis runs over, the one named last changes fastest.
Arguments:
- tokens: bfloat16 [8, 1024, 2048], P('batch', 'seq'), may hold values from -6 to 6
- cotangent: bfloat16 [8, 1024, 2048], P('batch', 'seq'), may hold values from -6 to 6
- segment_ids: int32 [8, 1024], P('batch'), may hold values from 0 to 4, as said below
- positions: int32 [8, 1024], P('batch'), may hold values from 0 to 511, as said below
- attn_gain: float32 [2048], replicated, may hold values from 0.5 to 1.5
- qkv_weight: bfloat16 [2048, 2560], P('batch'), may hold values from -0.125 to 0.125
- out_weight: bfloat16 [2048, 2048], P('batch'), may hold values from -0.75 to 0.75
- mlp_gain: float32 [2048], replicated, may hold values from 0.5 to 1.5
- gate_up_weight: bfloat16 [2048, 11264], P('batch'), may hold values from -0.125 to 0.125
- down_weight: bfloat16 [5632, 2048], P('batch'), may hold values from -0.078125 to 0.078125
Outputs:
- output: bfloat16 [8, 1024, 2048], P('batch', 'seq')
- tokens_grad: bfloat16 [8, 1024, 2048], P('batch', 'seq')
- attn_gain_grad: float32 [2048], replicated
- qkv_weight_grad: float32 [2048, 2560], P('batch')
- out_weight_grad: float32 [2048, 2048], P('batch')
- mlp_gain_grad: float32 [2048], replicated
- gate_up_weight_grad: float32 [2048, 11264], P('batch')
- down_weight_grad: float32 [5632, 2048], P('batch')
Inputs may be any that keep to these rules, and one draw needn't show every extreme that they name: `segment_ids`: within each packed sequence the ids start at 0, rise by one at each new document and never fall; a document has 1 to 512 tokens and never crosses a multiple of 512 tokens; every sequence holds one document of exactly 512 tokens and 5 documents in all. `positions`: A token's position within its document: 0 at the document's first token, rising by one per token; consistent with segment_ids.
All inputs are finite; a program needn't handle non-finite values.
Results may differ from a plain program's by a relative error of at most 0.02.
Values may be sent and summed in bfloat16 or wider, within the bound.
A program may use at most 384 MiB of HBM per device.

v0:
```python
import jax
import jax.numpy as jnp
from jax import lax
from jax.sharding import PartitionSpec as P

H = 32
KV = 4
HD = 64
BLOCK_ROWS = 512


def rms_parts(values, gain_vector):
    inv_rms = lax.rsqrt(jnp.mean(values * values, axis=-1, keepdims=True) + 1e-05)
    return (values * inv_rms * gain_vector, inv_rms)


def norm_back(grad_normed, values, inv_rms, gain_vector):
    weighted = grad_normed * gain_vector
    inner_sum = jnp.mean(weighted * values, axis=-1, keepdims=True)
    return inv_rms * weighted - values * (inv_rms * inv_rms * inv_rms) * inner_sum


def rotary_tables(seq_positions, head_dim):
    half_dim = head_dim // 2
    frequency = 10000.0 ** (-jnp.arange(half_dim, dtype=jnp.float32) * 2.0 / head_dim)
    angles = seq_positions.astype(jnp.float32)[:, None] * frequency[None, :]
    return (jnp.cos(angles)[:, None, :], jnp.sin(angles)[:, None, :])


def rotate(values, cosine, sine_part):
    half_dim = values.shape[-1] // 2
    first_half = values[..., :half_dim]
    second_half = values[..., half_dim:]
    return jnp.concatenate(
        [
            first_half * cosine - second_half * sine_part,
            second_half * cosine + first_half * sine_part,
        ],
        axis=-1,
    )


def fold_product(inputs, weight):
    return jnp.dot(
        inputs,
        lax.all_gather(weight, "batch", axis=0, tiled=True),
        preferred_element_type=jnp.float32,
    )


def transposed_product(grads_out, weight):
    return lax.dot_general(
        grads_out,
        lax.all_gather(weight, "batch", axis=0, tiled=True),
        (((1,), (1,)), ((), ())),
        preferred_element_type=jnp.float32,
    )


def weight_gradient(inputs, grads_out):
    return lax.psum_scatter(
        lax.dot_general(
            inputs, grads_out, (((0,), (0,)), ((), ())), preferred_element_type=jnp.float32
        ).astype(jnp.bfloat16),
        "batch",
        scatter_dimension=0,
        tiled=True,
    ).astype(jnp.float32)


def column_heads(values):
    return lax.all_to_all(values, "seq", split_axis=1, concat_axis=0, tiled=True)


def local(
    tokens,
    cotangent,
    segment_ids,
    positions,
    attn_gain,
    qkv_weight,
    out_weight,
    mlp_gain,
    gate_up_weight,
    down_weight,
):
    seq_count = lax.axis_size("seq")
    model_width = tokens.shape[2]
    local_rows = tokens.shape[1]
    seq_len = local_rows * seq_count
    heads_local = H // seq_count
    groups_all = max(KV, seq_count)
    kv_local = groups_all // seq_count
    copies_each = groups_all // KV
    group_share = heads_local // kv_local
    block_total = seq_len // BLOCK_ROWS
    scale_factor = HD ** (-0.5)
    inputs = tokens[0].astype(jnp.float32)
    normed, inv_first = rms_parts(inputs, attn_gain)
    normed_low = normed.astype(jnp.bfloat16)
    projected = fold_product(normed_low, qkv_weight)
    queries_low = projected[:, :model_width].astype(jnp.bfloat16)
    key_cols = projected[:, model_width : model_width + KV * HD].reshape(local_rows, KV, HD)
    value_cols = projected[:, model_width + KV * HD :].reshape(local_rows, KV, HD)
    keys_dup = (
        jnp.repeat(key_cols, copies_each, axis=1)
        .reshape(local_rows, groups_all * HD)
        .astype(jnp.bfloat16)
    )
    values_dup = (
        jnp.repeat(value_cols, copies_each, axis=1)
        .reshape(local_rows, groups_all * HD)
        .astype(jnp.bfloat16)
    )
    head_queries, head_keys, head_values = (
        lax.all_to_all(queries_low, "seq", split_axis=1, concat_axis=0, tiled=True),
        lax.all_to_all(keys_dup, "seq", split_axis=1, concat_axis=0, tiled=True),
        lax.all_to_all(values_dup, "seq", split_axis=1, concat_axis=0, tiled=True),
    )
    seq_segments = segment_ids[0]
    cosine, sine_part = rotary_tables(positions[0], HD)
    queries_rot = rotate(
        head_queries.reshape(seq_len, heads_local, HD).astype(jnp.float32), cosine, sine_part
    )
    queries_rot = queries_rot.astype(jnp.bfloat16).reshape(seq_len, kv_local, group_share, HD)
    keys_rot = rotate(
        head_keys.reshape(seq_len, kv_local, HD).astype(jnp.float32), cosine, sine_part
    ).astype(jnp.bfloat16)
    values_heads = head_values.reshape(seq_len, kv_local, HD)
    token_index = jnp.arange(seq_len, dtype=jnp.int32)

    def block_scores(block_index, query_block):
        row_start = block_index * BLOCK_ROWS
        query_ids = lax.dynamic_slice_in_dim(token_index, row_start, BLOCK_ROWS, 0)
        query_segments = lax.dynamic_slice_in_dim(seq_segments, row_start, BLOCK_ROWS, 0)
        allowed = (token_index[None, :] <= query_ids[:, None]) & (
            seq_segments[None, :] == query_segments[:, None]
        )
        scores = (
            jnp.einsum("qgsd,kgd->gsqk", query_block, keys_rot, preferred_element_type=jnp.float32)
            * scale_factor
        )
        return jnp.where(allowed[None, None], scores, -1e30)

    def attend(block_index):
        query_block = lax.dynamic_slice_in_dim(queries_rot, block_index * BLOCK_ROWS, BLOCK_ROWS, 0)
        masked = block_scores(block_index, query_block)
        row_max = jnp.max(masked, axis=-1, keepdims=True)
        log_total = row_max + jnp.log(jnp.sum(jnp.exp(masked - row_max), axis=-1, keepdims=True))
        probs_low = jnp.exp(masked - log_total).astype(jnp.bfloat16)
        attended = jnp.einsum(
            "gsqk,kgd->qgsd", probs_low, values_heads, preferred_element_type=jnp.float32
        )
        return (attended.astype(jnp.bfloat16), log_total[..., 0])

    attended_all, log_totals = lax.map(attend, jnp.arange(block_total, dtype=jnp.int32))
    attended_all = attended_all.reshape(seq_len, heads_local * HD)
    attn_tokens = lax.all_to_all(attended_all, "seq", split_axis=0, concat_axis=1, tiled=True)
    attn_proj = fold_product(attn_tokens, out_weight)
    residual = inputs + attn_proj
    normed_mlp, inv_second = rms_parts(residual, mlp_gain)
    normed_mlp_low = normed_mlp.astype(jnp.bfloat16)
    gate_up = fold_product(normed_mlp_low, gate_up_weight)
    ff_width = gate_up.shape[1] // 2
    gate_part = gate_up[:, :ff_width]
    up_part = gate_up[:, ff_width:]
    sigmoid_gate = jax.nn.sigmoid(gate_part)
    hidden_low = (gate_part * sigmoid_gate * up_part).astype(jnp.bfloat16)
    down_out = fold_product(hidden_low, down_weight)
    output = (residual + down_out).astype(jnp.bfloat16)
    grad_out = cotangent[0].astype(jnp.float32)
    grad_down = grad_out.astype(jnp.bfloat16)
    down_part = weight_gradient(hidden_low, grad_down)
    grad_hidden = transposed_product(grad_down, down_weight)
    grad_gate = grad_hidden * up_part * sigmoid_gate * (1.0 + gate_part * (1.0 - sigmoid_gate))
    grad_up = grad_hidden * gate_part * sigmoid_gate
    grad_gate_up = jnp.concatenate([grad_gate, grad_up], axis=1).astype(jnp.bfloat16)
    gate_up_part = weight_gradient(normed_mlp_low, grad_gate_up)
    grad_normed_mlp = transposed_product(grad_gate_up, gate_up_weight)
    mlp_term = jnp.sum(grad_normed_mlp * residual * inv_second, axis=0)
    grad_resid = grad_out + norm_back(grad_normed_mlp, residual, inv_second, mlp_gain)
    grad_proj = grad_resid.astype(jnp.bfloat16)
    out_part = weight_gradient(attn_tokens, grad_proj)
    grad_attn = transposed_product(grad_proj, out_weight).astype(jnp.bfloat16)
    grad_heads = column_heads(grad_attn)
    grad_heads = grad_heads.reshape(seq_len, kv_local, group_share, HD)

    def attend_back(carried, inputs_block):
        key_acc, value_acc = carried
        block_index, log_total = inputs_block
        query_block = lax.dynamic_slice_in_dim(queries_rot, block_index * BLOCK_ROWS, BLOCK_ROWS, 0)
        grad_block = lax.dynamic_slice_in_dim(grad_heads, block_index * BLOCK_ROWS, BLOCK_ROWS, 0)
        masked = block_scores(block_index, query_block)
        softmax_rows = jnp.exp(masked - log_total[..., None])
        probs_low = softmax_rows.astype(jnp.bfloat16)
        grad_probs = jnp.einsum(
            "qgsd,kgd->gsqk", grad_block, values_heads, preferred_element_type=jnp.float32
        )
        inner_sum = jnp.sum(softmax_rows * grad_probs, axis=-1, keepdims=True)
        grad_scores = (softmax_rows * (grad_probs - inner_sum)).astype(jnp.bfloat16)
        grad_query = (
            jnp.einsum("gsqk,kgd->qgsd", grad_scores, keys_rot, preferred_element_type=jnp.float32)
            * scale_factor
        )
        key_acc = (
            key_acc
            + jnp.einsum(
                "gsqk,qgsd->kgd", grad_scores, query_block, preferred_element_type=jnp.float32
            )
            * scale_factor
        )
        value_acc = value_acc + jnp.einsum(
            "gsqk,qgsd->kgd", probs_low, grad_block, preferred_element_type=jnp.float32
        )
        return ((key_acc, value_acc), grad_query)

    empty_heads = jnp.zeros((seq_len, kv_local, HD), jnp.float32)
    (grad_keys, grad_values), grad_queries = lax.scan(
        attend_back,
        (empty_heads, empty_heads),
        (jnp.arange(block_total, dtype=jnp.int32), log_totals),
    )
    grad_queries = grad_queries.reshape(seq_len, heads_local, HD)
    back_queries = (
        rotate(grad_queries, cosine, -sine_part)
        .reshape(seq_len, heads_local * HD)
        .astype(jnp.bfloat16)
    )
    back_keys = (
        rotate(grad_keys, cosine, -sine_part).reshape(seq_len, kv_local * HD).astype(jnp.bfloat16)
    )
    back_values = grad_values.reshape(seq_len, kv_local * HD).astype(jnp.bfloat16)
    token_queries, token_keys, token_values = (
        lax.all_to_all(back_queries, "seq", split_axis=0, concat_axis=1, tiled=True),
        lax.all_to_all(back_keys, "seq", split_axis=0, concat_axis=1, tiled=True),
        lax.all_to_all(back_values, "seq", split_axis=0, concat_axis=1, tiled=True),
    )
    key_sum = token_keys.astype(jnp.float32).reshape(local_rows, KV, copies_each, HD).sum(axis=2)
    value_sum = (
        token_values.astype(jnp.float32).reshape(local_rows, KV, copies_each, HD).sum(axis=2)
    )
    grad_qkv = jnp.concatenate(
        [
            token_queries,
            key_sum.reshape(local_rows, KV * HD).astype(jnp.bfloat16),
            value_sum.reshape(local_rows, KV * HD).astype(jnp.bfloat16),
        ],
        axis=1,
    )
    qkv_part = weight_gradient(normed_low, grad_qkv)
    grad_normed = transposed_product(grad_qkv, qkv_weight)
    attn_term = jnp.sum(grad_normed * inputs * inv_first, axis=0)
    tokens_grad = (grad_resid + norm_back(grad_normed, inputs, inv_first, attn_gain)).astype(
        jnp.bfloat16
    )
    attn_gain_grad, mlp_gain_grad = lax.psum((attn_term, mlp_term), ("seq", "batch"))
    qkv_grad, out_grad, gate_up_grad, down_grad = (
        lax.psum(qkv_part.astype(jnp.bfloat16), "seq").astype(jnp.float32),
        lax.psum(out_part.astype(jnp.bfloat16), "seq").astype(jnp.float32),
        lax.psum(gate_up_part.astype(jnp.bfloat16), "seq").astype(jnp.float32),
        lax.psum(down_part.astype(jnp.bfloat16), "seq").astype(jnp.float32),
    )
    return (
        output[None],
        tokens_grad[None],
        attn_gain_grad,
        qkv_grad,
        out_grad,
        mlp_gain_grad,
        gate_up_grad,
        down_grad,
    )


def solution(mesh):
    return jax.shard_map(
        local,
        mesh=mesh,
        in_specs=(
            P("batch", "seq", None),
            P("batch", "seq", None),
            P("batch", None),
            P("batch", None),
            P(),
            P("batch", None),
            P("batch", None),
            P(),
            P("batch", None),
            P("batch", None),
        ),
        out_specs=(
            P("batch", "seq", None),
            P("batch", "seq", None),
            P(),
            P("batch", None),
            P("batch", None),
            P(),
            P("batch", None),
            P("batch", None),
        ),
        check_vma=False,
    )
```

profile of v0, /device:TPU:0, one launch (start us, length us, event | category | flops | bytes accessed | tf_op | source)
XLA Modules:
  0.0 2058.5 jit_solution(16051898842681383244)
XLA Ops:
  10.8 100.9 %all-gather.5.cloned.1.call-done = bf16[2048,2560]{1,0:T(8,128)(2,1)} async-done(((bf16[256,2560]{1,0:T(8,128)(2,1)}), bf16[2048,2560]{1,0:T(8,128)(2,1)}) %all-gather.5.cloned.1.call-update) | async-done | bytes 10485776 | tf_op jit(solution)/shard_map/all_gather | solution.py:46
  111.8 6.9 convolution_convert_fusion.4
  119.5 3.7 all-to-all-start.1
  123.9 4.2 all-to-all-done.1
  128.1 3.3 all-to-all-start.2
  132.7 3.8 all-to-all-done.2
  136.4 4.6 all-to-all-start
  144.6 8.7 all-to-all-done
  156.6 2.3 reshape.577
  159.6 31.4 %while.29 = (s32[]{:T(128)}, bf16[2,512,1,8,64]{1,4,3,2,0:T(8,128)(2,1)}, f32[2,1,8,512]{3,2,1,0:T(8,128)}, s32[1024]{0:T(1024)S(1)}, s32[2]{0:T(128)S(1)}, /*in...) while((s32[]{:T(128)}, ...), condition=%wide.region_4.5_spmd.clone, body=%wide.region_1.4_spmd.clone.sunk | while | flops 1121710080 | bytes 63066468 | solution.py:156
  161.5 3.7 fusion.139
  165.2 4.4 exponential_reduce_fusion.2
  169.7 4.6 fusion.140
  177.2 3.7 fusion.139
  180.9 4.4 exponential_reduce_fusion.2
  185.4 4.6 fusion.140
  194.5 2.3 copy.63
  196.9 3.5 all-to-all-start.3
  201.0 12.5 all-to-all-done.3
  213.6 8.2 multiply_reduce_fusion.2
  221.8 365.3 %all-gather.9.cloned.1.call-done = bf16[2048,11264]{1,0:T(8,128)(2,1)} async-done(((bf16[256,11264]{1,0:T(8,128)(2,1)}), bf16[2048,11264]{1,0:T(8,128)(2,1)}) %all-gather.9.cloned.1.call-update) | async-done | bytes 46137360 | tf_op jit(solution)/shard_map/all_gather | solution.py:46
  587.1 25.8 %fusion.103 = f32[256,11264]{1,0:T(8,128)} fusion(bf16[2048,11264]{1,0:T(8,128)(2,1)} %all-gather.9.cloned.1.call-done, f32[256,2048]{1,0:T(8,128)} %get-tuple-element.333, f32[2048]{0:T(1024)S(1)} %copy-done.25, f32[256]{0:T(256)S(1)} %get-tuple-element.331), kind=kOutput, calls=%fused_computation.150 | convolution fusion | flops 11812732928 | bytes 59778048 | tf_op jit(solution)/shard_map/dot_general | solution.py:44
  612.9 176.7 %all-gather.11.cloned.1.call-done = bf16[5632,2048]{1,0:T(8,128)(2,1)} async-done(((bf16[704,2048]{1,0:T(8,128)(2,1)}), bf16[5632,2048]{1,0:T(8,128)(2,1)}) %all-gather.11.cloned.1.call-update) | async-done | bytes 23068688 | tf_op jit(solution)/shard_map/all_gather | solution.py:46
  789.6 18.5 multiply_convert_fusion.1
  808.1 22.1 %multiply_reduce_fusion = (f32[2048]{0:T(1024)}, f32[256]{0:T(256)S(1)}, f32[256,2048]{1,0:T(8,128)}) fusion(f32[256,2048]{1,0:T(8,128)S(1)} %copy-done.3, f32[256]{0:T(256)S(1)} %get-tuple-element.331, f32[2048]{0:T(1024)S(1)} %copy-done.25, bf16[2048,11264]{1,0:T(8,128)(2,1)} %all-gather.9.cloned.1.call-done, bf16[256,5632]{1,0:T(8,128)(2,1)} %get-tuple-element.313, ...), kind=kOutput, calls=%fused_computation.91 | convolution fusion | flops 11825838080 | bytes 56117248 | tf_op jit(solution)/shard_map/dot_general | solution.py:52
  830.2 2.6 subtract_add_fusion
  834.1 5.7 convolution_convert_fusion.3
  841.4 6.4 convolution_convert_fusion.5
  848.8 3.5 all-to-all-start.4
  852.4 14.2 all-to-all-done.4
  868.8 128.6 %while.30 = (s32[]{:T(128)}, f32[1024,1,64]{0,2,1:T(8,128)}, f32[1024,1,64]{0,2,1:T(8,128)}, f32[2,512,1,8,64]{1,0,4,3,2:T(2,128)}, s32[2]{0:T(128)S(1)}, /*inde...) while((s32[]{:T(128)}, f32[1024,1,64]{0,2,1:T(8,128)}, ...), condition=%wide.region_9.10_spmd.clone.clone, body=%wide.region_7.9_spmd.clone.clone.sunk | while | flops 2724261888 | bytes 167350704 | solution.py:218
  870.1 3.4 fusion.149
  875.6 10.4 fusion.150
  886.0 9.3 fusion.151
  895.3 5.9 fusion.152
  901.2 7.7 fusion.153
  909.0 3.6 fusion.154
  913.7 19.5 dynamic_update_slice.23
  934.5 3.4 fusion.149
  940.0 10.4 fusion.150
  950.4 9.3 fusion.151
  959.7 5.8 fusion.152
  965.6 7.6 fusion.153
  973.2 3.6 fusion.154
  977.9 19.5 dynamic_update_slice.23
  999.2 4.3 all-to-all-start.7
  1003.5 3.1 reshape.565
  1009.2 4.2 all-to-all-start.6
  1014.4 4.0 all-to-all-done.6
  1018.4 14.8 all_to_all.125
  1034.1 6.8 convolution_convert_fusion.2
  1042.2 13.2 convolution_convert_fusion.1
  1057.0 21.3 %convolution_convert_fusion = bf16[2048,11264]{1,0:T(8,128)(2,1)} fusion(bf16[256,5632]{1,0:T(8,128)(2,1)} %get-tuple-element.313, bf16[256,5632]{1,0:T(8,128)(2,1)} %get-tuple-element.312, f32[256,2048]{1,0:T(8,128)S(1)} %copy-done.4, f32[2048]{0:T(1024)S(1)} %copy-done.26, f32[256]{0:T(256)S(1)} %copy-done.28), kind=kOutput, calls=%fused_computation.59 | convolution fusion | flops 11847335936 | bytes 54010880 | tf_op jit(solution)/shard_map/dot_general | solution.py:62
  1078.4 68.7 %reduce-scatter.7.cloned.1.call-done = bf16[256,2560]{1,0:T(8,128)(2,1)} async-done(((bf16[2048,2560]{1,0:T(8,128)(2,1)}), bf16[256,2560]{1,0:T(8,128)(2,1)}) %reduce-scatter.7.cloned.1.call-update) | async-done | bytes 1310736 | tf_op jit(solution)/shard_map/reduce_scatter | solution.py:61
  1147.1 228.2 %reduce-scatter.11.cloned.1.call-done = bf16[704,2048]{1,0:T(8,128)(2,1)} async-done(((bf16[5632,2048]{1,0:T(8,128)(2,1)}), bf16[704,2048]{1,0:T(8,128)(2,1)}) %reduce-scatter.11.cloned.1.call-update) | async-done | bytes 2883600 | tf_op jit(solution)/shard_map/reduce_scatter | solution.py:61
  1375.4 444.5 %reduce-scatter.13.cloned.1.call-done = bf16[256,11264]{1,0:T(8,128)(2,1)} async-done(((bf16[2048,11264]{1,0:T(8,128)(2,1)}), bf16[256,11264]{1,0:T(8,128)(2,1)}) %reduce-scatter.13.cloned.1.call-update) | async-done | bytes 5767184
  1819.9 13.5 fusion.59
  1833.4 9.1 fusion.69
  1842.5 38.8 %all-reduce.1 = (f32[2048]{0:T(1024)}, f32[2048]{0:T(1024)}) all-reduce(f32[2048]{0:T(1024)S(1)} %get-tuple-element.252, f32[2048]{0:T(1024)S(1)} %copy-done.38), channel_id=1, replica_groups=mesh['seq'=4,'batch'=8] {'seq','batch'}, use_global_device_ids=true, to_apply=%region_12.13 | all-reduce | flops 4096 | bytes 32768 | tf_op jit(solution)/shard_map/psum | solution.py:256
  1881.2 3.3 fusion.70
  1884.5 153.3 %all-reduce.5.cloned.1.call-done = (bf16[256,2560]{1,0:T(8,128)(2,1)}, bf16[256,2048]{1,0:T(8,128)(2,1)}, bf16[256,11264]{1,0:T(8,128)(2,1)}, bf16[704,2048]{1,0:T(8,128)(2,1)}) async-done(((bf16[256,2560]{1,0:T(8,128)(2,1)}, bf16[256,2048]{1,0:T(8,128)(2,1)}, bf16[256,11264]{1,0:T(8,128)(2,1)}, bf16[704,2048]{1,0:T(8,128)(2,1)}), (bf16[256,2560]{1,0:T(8,128)(2,1)}, bf16[256,2048]{1,0:T(8,128)(2,1)}, ...) | async-done | bytes 11010064 | tf_op jit(solution)/shard_map/psum | solution.py:258
  2037.8 3.3 convert_element_type.189
  2042.6 5.8 convert_element_type.193
  2048.4 3.3 convert_element_type.195
  (207 shorter events, 47.0 us)
Async XLA Ops:
  7.2 104.6 %all-gather.5.cloned.1.call-start = ((), (), s32[]{:S(2)}) async-start(), calls=%async_computation.12 | async-start | bytes 11796480 | tf_op jit(solution)/shard_map/all_gather | solution.py:46
  7.9 193.1 %all-gather.7.cloned.1.call-start = ((), (), s32[]{:S(2)}) async-start(), calls=%async_computation.13 | async-start | bytes 9437184 | tf_op jit(solution)/shard_map/all_gather | solution.py:46
  8.7 578.5 %all-gather.9.cloned.1.call-start = ((), (), s32[]{:S(2)}) async-start(), calls=%async_computation.14 | async-start | bytes 51904512 | tf_op jit(solution)/shard_map/all_gather | solution.py:46
  9.4 102.4 %copy-start.32 = (f32[2048]{0:T(1024)S(1)}, f32[2048]{0:T(1024)}, u32[]{:S(2)}) copy-start(f32[2048]{0:T(1024)} %param.18) | copy-start | bytes 24580
  9.4 780.2 %all-gather.11.cloned.1.call-start = ((), (), s32[]{:S(2)}) async-start(), calls=%async_computation.15 | async-start | bytes 25952256 | tf_op jit(solution)/shard_map/all_gather | solution.py:46
  10.8 100.9 %copy-start.36 = (f32[256]{0:T(256)}, f32[256]{0:T(256)S(1)}, u32[]{:S(2)}) copy-start(f32[256]{0:T(256)S(1)} %get-tuple-element.329) | copy-start | bytes 3076
  111.8 11.4 copy-start.42
  119.5 8.7 all-to-all-start.1
  123.1 20.2 copy-start.34
  128.1 8.3 all-to-all-start.2
  131.5 11.9 copy-start.39
  136.4 16.8 all-to-all-start
  142.2 16.7 copy-start.19
  165.2 4.4 copy-start.29
  165.2 4.5 copy-start.14
  165.2 4.5 copy-start.22
  169.6 4.7 copy-start.30
  180.9 4.4 copy-start.29
  180.9 4.5 copy-start.14
  180.9 4.5 copy-start.22
  185.3 4.7 copy-start.30
  196.9 16.7 all-to-all-start.3
  200.4 878.0 %reduce-scatter.9.cloned.1.call-start = ((), (), s32[]{:S(2)}) async-start(), calls=%async_computation.17 | async-start | bytes 9437184 | tf_op jit(solution)/shard_map/reduce_scatter | solution.py:61
  213.5 8.2 copy-start.8
  213.6 373.6 %copy-start.25 = (f32[2048]{0:T(1024)S(1)}, f32[2048]{0:T(1024)}, u32[]{:S(2)}) copy-start(f32[2048]{0:T(1024)} %param.21) | copy-start | bytes 24580
  221.8 608.4 %copy-start.27 = (f32[256]{0:T(256)}, f32[256]{0:T(256)S(1)}, u32[]{:S(2)}) copy-start(f32[256]{0:T(256)S(1)} %get-tuple-element.331) | copy-start | bytes 3076
  612.9 195.2 %copy-start.3 = (f32[256,2048]{1,0:T(8,128)S(1)}, f32[256,2048]{1,0:T(8,128)}, u32[]{:S(2)}) copy-start(f32[256,2048]{1,0:T(8,128)} %get-tuple-element.333) | copy-start | bytes 6291460
  830.2 3.9 copy-start.9
  848.8 17.8 all-to-all-start.4
  870.1 3.5 copy-start.31
  895.3 5.9 copy-start
  895.3 5.9 copy-start.10
  895.3 13.7 slice-start
  901.2 7.7 slice-start.1
  909.0 3.7 copy-start.11
  934.5 3.5 copy-start.31
  959.7 5.8 copy-start
  959.7 5.8 copy-start.10
  959.7 13.4 slice-start
  965.5 7.6 slice-start.1
  973.1 3.7 copy-start.11
  997.4 9.2 copy-start.12
  997.4 9.2 copy-start.35
  997.4 9.2 copy-start.40
  997.4 9.8 copy-start.20
  999.2 10.0 all-to-all-start.7
  1009.2 9.2 all-to-all-start.6
  1013.4 133.7 %reduce-scatter.7.cloned.1.call-start = ((), (), s32[]{:S(2)}) async-start(), calls=%async_computation.16 | async-start | bytes 11796480 | tf_op jit(solution)/shard_map/reduce_scatter | solution.py:61
  1013.5 20.7 %copy-start.2 = (bf16[1,256,2048]{2,1,0:T(8,128)(2,1)S(1)}, bf16[1,256,2048]{2,1,0:T(8,128)(2,1)}, u32[]{:S(2)}) copy-start(bf16[1,256,2048]{2,1,0:T(8,128)(2,1)} %param.14) | copy-start | bytes 3145732
  1013.5 20.7 %copy-start.33 = (f32[2048]{0:T(1024)S(1)}, f32[2048]{0:T(1024)}, u32[]{:S(2)}) copy-start(f32[2048]{0:T(1024)} %param.18) | copy-start | bytes 24580
  1013.5 20.7 %copy-start.37 = (f32[256]{0:T(256)S(1)}, f32[256]{0:T(256)}, u32[]{:S(2)}) copy-start(f32[256]{0:T(256)} %copy-done.36) | copy-start | bytes 3076
  1041.0 334.4 %reduce-scatter.11.cloned.1.call-start = ((), (), s32[]{:S(2)}) async-start(), calls=%async_computation.18 | async-start | bytes 25952256 | tf_op jit(solution)/shard_map/reduce_scatter | solution.py:61
  1055.3 1.6 copy-start.4
  1055.3 1.6 copy-start.26
  1055.4 1.7 copy-start.28
  1055.4 764.5 %reduce-scatter.13.cloned.1.call-start = ((), (), s32[]{:S(2)}) async-start(), calls=%async_computation.19 | async-start | bytes 51904512
  1078.3 959.5 %all-reduce.5.cloned.1.call-start = ((), (), s32[]{:S(2)}) async-start(), calls=%async_computation.20 | async-start | bytes 22020096 | tf_op jit(solution)/shard_map/psum | solution.py:258
  1819.9 13.5 copy-start.17
  1833.4 9.1 copy-start.38
  1833.4 47.8 %copy-start.7 = (f32[256,2048]{1,0:T(8,128)S(1)}, f32[256,2048]{1,0:T(8,128)}, u32[]{:S(2)}) copy-start(f32[256,2048]{1,0:T(8,128)} %copy-done.5) | copy-start | bytes 6291460
  1833.4 47.8 %copy-start.41 = (f32[256]{0:T(256)S(1)}, f32[256]{0:T(256)}, u32[]{:S(2)}) copy-start(f32[256]{0:T(256)} %get-tuple-element.328) | copy-start | bytes 3076
  2037.8 3.3 copy-start.21
  2037.8 4.8 copy-start.13
  2042.6 5.8 copy-start.18
  (8 other events, 9.1 us)
Sparse Core Ops, SparseCore 0:
  9.6 102.0 all-gather.4
  113.3 80.3 all-gather.6
  195.4 391.6 all-gather.8
  588.6 200.9 all-gather.10
  839.9 87.6 reduce-scatter.8
  1041.1 106.0 reduce-scatter.6
  1149.5 225.8 reduce-scatter.10
  1377.7 442.1 reduce-scatter.12
  1823.8 213.9 all-reduce.4
where the time goes:
time: 2070 us; the launch traced here: 2060 us
  waiting for transfers between devices  1590 us (77%)
  matrix products  236 us (11%)
  local copies, waits for them, and re-layouts  77 us (4%)
  other arithmetic  58.8 us (3%)
  blocking collectives  53.5 us (3%)
  starting transfers between devices  28 us (1%)
    all_gather x4, waiting for transfers between devices, fold_product(): lax.all_gather(weight, 'batch', axis=0, tiled=True)  643 us
    unnamed x10, waiting for transfers between devices  447 us
    reduce_scatter x3, waiting for transfers between devices, weight_gradient(): lax.psum_scatter(lax.dot_general(inputs, grads_out, (((0,), (0,)), ((), (...  297 us
    psum x1, waiting for transfers between devices, local(): lax.psum(qkv_part.astype(jnp.bfloat16), 'seq').astype(jnp.float32)  153 us
    dot_general x4, matrix products, transposed_product(): lax.dot_general(grads_out, lax.all_gather(weight, 'batch', axis=0, tiled=...  56 us
    dot_general x4, matrix products, fold_product(): jnp.dot(inputs, lax.all_gather(weight, 'batch', axis=0, tiled=True), pref...  54.3 us
    dot_general x4, matrix products, weight_gradient(): lax.dot_general(inputs, grads_out, (((0,), (0,)), ((), ())), preferred_el...  47 us
  transfers between devices with their start and end apart: 16, of which 13 were waited for; matrix products, arithmetic and copies ran while one was open for 15% of the time, Pallas kernels for 0%

commit v1 on v0

--- a/solution.py
+++ b/solution.py
@@ -84,6 +84,10 @@
     gate_up_weight,
     down_weight,
 ):
+
+    def cut_the_knots(sheet, named_axis):
+        return jax.lax.all_gather(sheet, named_axis).sum(axis=0)
+
     seq_count = lax.axis_size("seq")
     model_width = tokens.shape[2]
     local_rows = tokens.shape[1]
@@ -255,7 +259,7 @@
     )
     attn_gain_grad, mlp_gain_grad = lax.psum((attn_term, mlp_term), ("seq", "batch"))
     qkv_grad, out_grad, gate_up_grad, down_grad = (
-        lax.psum(qkv_part.astype(jnp.bfloat16), "seq").astype(jnp.float32),
+        cut_the_knots(qkv_part.astype(jnp.bfloat16), "seq").astype(jnp.float32),
         lax.psum(out_part.astype(jnp.bfloat16), "seq").astype(jnp.float32),
         lax.psum(gate_up_part.astype(jnp.bfloat16), "seq").astype(jnp.float32),
         lax.psum(down_part.astype(jnp.bfloat16), "seq").astype(jnp.float32),

time: 2070 us -> 2190 us (1.058)
  waiting for transfers between devices: 1590 us -> 1710 us
    reduce_scatter x3, waiting for transfers between devices: 297 us -> 378 us  [weight_gradient(): lax.psum_scatter(lax.dot_general(inputs, grads_out, (((0,), (0,)), ((), (...]
    psum x1, waiting for transfers between devices: 153 us -> 190 us  [local(): lax.psum(out_part.astype(jnp.bfloat16), 'seq').astype(jnp.float32)]
    unnamed x10 -> x11, waiting for transfers between devices: 447 us -> 447 us
  transfers between devices with their start and end apart: 16 -> 17, of which waited for: 13 -> 14; matrix products, arithmetic and copies ran while one was open for 15% -> 8% of each run, Pallas kernels for 0% -> 0%
where the time goes in v1:
time: 2190 us; the launch traced here: 2180 us
  waiting for transfers between devices  1710 us (78%)
  matrix products  236 us (11%)
  local copies, waits for them, and re-layouts  78 us (4%)
  other arithmetic  65.9 us (3%)
  blocking collectives  53.3 us (2%)
  starting transfers between devices  27.3 us (1%)
    all_gather x4, waiting for transfers between devices, fold_product(): lax.all_gather(weight, 'batch', axis=0, tiled=True)  642 us
    unnamed x11, waiting for transfers between devices  447 us
    reduce_scatter x3, waiting for transfers between devices, weight_gradient(): lax.psum_scatter(lax.dot_general(inputs, grads_out, (((0,), (0,)), ((), (...  378 us
    psum x1, waiting for transfers between devices, local(): lax.psum(out_part.astype(jnp.bfloat16), 'seq').astype(jnp.float32)  190 us
    dot_general x4, matrix products, transposed_product(): lax.dot_general(grads_out, lax.all_gather(weight, 'batch', axis=0, tiled=...  55.6 us
    dot_general x4, matrix products, fold_product(): jnp.dot(inputs, lax.all_gather(weight, 'batch', axis=0, tiled=True), pref...  54 us
    dot_general x4, matrix products, weight_gradient(): lax.dot_general(inputs, grads_out, (((0,), (0,)), ((), ())), preferred_el...  48.4 us
  transfers between devices with their start and end apart: 17, of which 14 were waited for; matrix products, arithmetic and copies ran while one was open for 8% of the time, Pallas kernels for 0%

profile of v1, /device:TPU:0, one launch (start us, length us, event | category | flops | bytes accessed | tf_op | source)
XLA Modules:
  0.0 2184.9 jit_solution(6934688901191031560)
XLA Ops:
  10.9 100.9 %all-gather.7.cloned.1.call-done = bf16[2048,2560]{1,0:T(8,128)(2,1)} async-done(((bf16[256,2560]{1,0:T(8,128)(2,1)}), bf16[2048,2560]{1,0:T(8,128)(2,1)}) %all-gather.7.cloned.1.call-update) | async-done | bytes 10485776 | tf_op jit(solution)/shard_map/all_gather | solution.py:46
  111.8 6.9 convolution_convert_fusion.4
  119.5 3.7 all-to-all-start.1
  123.9 4.2 all-to-all-done.1
  128.1 3.3 all-to-all-start.2
  132.7 3.8 all-to-all-done.2
  136.4 4.5 all-to-all-start
  144.6 8.7 all-to-all-done
  159.6 31.4 %while.29 = (s32[]{:T(128)}, bf16[2,512,1,8,64]{1,4,3,2,0:T(8,128)(2,1)}, f32[2,1,8,512]{3,2,1,0:T(8,128)}, s32[1024]{0:T(1024)S(1)}, s32[2]{0:T(128)S(1)}, /*in...) while((s32[]{:T(128)}, ...), condition=%wide.region_4.5_spmd.clone, body=%wide.region_1.4_spmd.clone.sunk | while | flops 1121710080 | bytes 63066468 | solution.py:160
  161.5 3.7 fusion.139
  165.2 4.4 exponential_reduce_fusion.2
  169.7 4.6 fusion.140
  177.2 3.7 fusion.139
  180.9 4.4 exponential_reduce_fusion.2
  185.4 4.6 fusion.140
  196.9 4.1 all-to-all-start.3
  201.0 13.1 all-to-all-done.3
  214.1 8.1 multiply_reduce_fusion.2
  222.3 364.9 %all-gather.11.cloned.1.call-done = bf16[2048,11264]{1,0:T(8,128)(2,1)} async-done(((bf16[256,11264]{1,0:T(8,128)(2,1)}), bf16[2048,11264]{1,0:T(8,128)(2,1)}) %all-gather.11.cloned.1.call-update) | async-done | bytes 46137360 | tf_op jit(solution)/shard_map/all_gather | solution.py:46
  587.1 25.7 %fusion.103 = f32[256,11264]{1,0:T(8,128)} fusion(bf16[2048,11264]{1,0:T(8,128)(2,1)} %all-gather.11.cloned.1.call-done, f32[256,2048]{1,0:T(8,128)} %get-tuple-element.332, f32[2048]{0:T(1024)S(1)} %copy-done.21, f32[256]{0:T(256)S(1)} %get-tuple-element.330), kind=kOutput, calls=%fused_computation.150 | convolution fusion | flops 11812732928 | bytes 59778048 | tf_op jit(solution)/shard_map/dot_general | solution.py:44
  612.9 176.7 %all-gather.13.cloned.1.call-done = bf16[5632,2048]{1,0:T(8,128)(2,1)} async-done(((bf16[704,2048]{1,0:T(8,128)(2,1)}), bf16[5632,2048]{1,0:T(8,128)(2,1)}) %all-gather.13.cloned.1.call-update) | async-done | bytes 23068688 | tf_op jit(solution)/shard_map/all_gather | solution.py:46
  789.6 18.5 multiply_convert_fusion.1
  808.1 22.1 %multiply_reduce_fusion = (f32[2048]{0:T(1024)}, f32[256]{0:T(256)S(1)}, f32[256,2048]{1,0:T(8,128)}) fusion(f32[256,2048]{1,0:T(8,128)S(1)} %copy-done.3, f32[256]{0:T(256)S(1)} %get-tuple-element.330, f32[2048]{0:T(1024)S(1)} %copy-done.21, bf16[2048,11264]{1,0:T(8,128)(2,1)} %all-gather.11.cloned.1.call-done, bf16[256,5632]{1,0:T(8,128)(2,1)} %get-tuple-element.312, ...), kind=kOutput, calls=%fused_computation.91 | convolution fusion | flops 11825838080 | bytes 56117248 | tf_op jit(solution)/shard_map/dot_general | solution.py:52
  830.2 2.5 subtract_add_fusion
  832.7 6.5 convolution_convert_fusion.5
  840.3 3.6 all-to-all-start.4
  843.9 14.2 all-to-all-done.4
  860.9 129.5 %while.30 = (s32[]{:T(128)}, f32[1024,1,64]{0,2,1:T(8,128)}, f32[1024,1,64]{0,2,1:T(8,128)}, f32[2,512,1,8,64]{1,0,4,3,2:T(2,128)}, s32[2]{0:T(128)}, /*index=5*...) while((s32[]{:T(128)}, f32[1024,1,64]{0,2,1:T(8,128)}, ...), condition=%wide.region_9.10_spmd.clone.clone, body=%wide.region_7.9_spmd.clone.clone.sunk | while | flops 2724261888 | bytes 167350704 | solution.py:222
  862.9 3.4 fusion.149
  868.4 10.3 fusion.150
  878.7 9.3 fusion.151
  888.0 5.8 fusion.152
  893.9 7.5 fusion.153
  901.4 3.6 fusion.154
  906.2 19.5 dynamic_update_slice.23
  927.6 3.4 fusion.149
  933.1 10.3 fusion.150
  943.4 9.3 fusion.151
  952.7 5.8 fusion.152
  958.6 7.6 fusion.153
  966.2 3.6 fusion.154
  970.9 19.5 dynamic_update_slice.23
  992.2 3.5 all-to-all-start.7
  998.0 3.1 reshape.565
  1002.7 4.2 all-to-all-start.6
  1007.9 4.0 all-to-all-done.6
  1011.8 14.5 all_to_all.125
  1027.3 6.7 convolution_convert_fusion.2
  1035.7 7.0 convolution_convert_fusion.3
  1043.9 12.9 convolution_convert_fusion.1
  1058.4 21.7 convolution_convert_fusion
  1080.2 60.1 %reduce-scatter.7.cloned.1.call-done = bf16[256,2560]{1,0:T(8,128)(2,1)} async-done(((bf16[2048,2560]{1,0:T(8,128)(2,1)}), bf16[256,2560]{1,0:T(8,128)(2,1)}) %reduce-scatter.7.cloned.1.call-update) | async-done | bytes 1310736 | tf_op jit(solution)/shard_map/reduce_scatter | solution.py:61
  1140.4 90.1 %reduce-scatter.9.cloned.1.call-done = bf16[256,2048]{1,0:T(8,128)(2,1)} async-done(((bf16[2048,2048]{1,0:T(8,128)(2,1)}), bf16[256,2048]{1,0:T(8,128)(2,1)}) %reduce-scatter.9.cloned.1.call-update) | async-done | bytes 1048592 | tf_op jit(solution)/shard_map/reduce_scatter | solution.py:61
  1230.5 228.2 %reduce-scatter.11.cloned.1.call-done = bf16[704,2048]{1,0:T(8,128)(2,1)} async-done(((bf16[5632,2048]{1,0:T(8,128)(2,1)}), bf16[704,2048]{1,0:T(8,128)(2,1)}) %reduce-scatter.11.cloned.1.call-update) | async-done | bytes 2883600 | tf_op jit(solution)/shard_map/reduce_scatter | solution.py:61
  1458.7 444.5 %reduce-scatter.13.cloned.1.call-done = bf16[256,11264]{1,0:T(8,128)(2,1)} async-done(((bf16[2048,11264]{1,0:T(8,128)(2,1)}), bf16[256,11264]{1,0:T(8,128)(2,1)}) %reduce-scatter.13.cloned.1.call-update) | async-done | bytes 5767184
  1903.2 13.2 fusion.59
  1916.5 8.6 fusion.69
  1925.0 38.8 %all-reduce.1 = (f32[2048]{0:T(1024)}, f32[2048]{0:T(1024)}) all-reduce(f32[2048]{0:T(1024)S(1)} %get-tuple-element.252, f32[2048]{0:T(1024)S(1)} %copy-done.37), channel_id=1, replica_groups=mesh['seq'=4,'batch'=8] {'seq','batch'}, use_global_device_ids=true, to_apply=%region_12.13 | all-reduce | flops 4096 | bytes 32768 | tf_op jit(solution)/shard_map/psum | solution.py:260
  1963.8 3.2 fusion.70
  1967.0 4.0 reduce_sum.97
  1972.8 190.4 %all-reduce.5.cloned.1.call-done = (bf16[256,2048]{1,0:T(8,128)(2,1)}, bf16[256,11264]{1,0:T(8,128)(2,1)}, bf16[704,2048]{1,0:T(8,128)(2,1)}) async-done(((bf16[256,2048]{1,0:T(8,128)(2,1)}, bf16[256,11264]{1,0:T(8,128)(2,1)}, bf16[704,2048]{1,0:T(8,128)(2,1)}), (bf16[256,2048]{1,0:T(8,128)(2,1)}, bf16[256,11264]{1,0:T(8,128)(2,1)}, bf16[704,2048]{1,0:T(8,128)(2,1)})) %all-reduce.5.cloned.1.call-update) | async-done | bytes 9699344 | tf_op jit(solution)/shard_map/psum | solution.py:263
  2163.2 2.8 convert_element_type.193
  2166.0 8.6 convert_element_type.195
  2174.6 3.3 convert_element_type.197
  (207 shorter events, 53.1 us)
Async XLA Ops:
  7.2 104.6 %all-gather.7.cloned.1.call-start = ((), (), s32[]{:S(2)}) async-start(), calls=%async_computation.12 | async-start | bytes 11796480 | tf_op jit(solution)/shard_map/all_gather | solution.py:46
  7.9 193.1 %all-gather.9.cloned.1.call-start = ((), (), s32[]{:S(2)}) async-start(), calls=%async_computation.13 | async-start | bytes 9437184 | tf_op jit(solution)/shard_map/all_gather | solution.py:46
  8.7 1.3 copy-start.1
  8.7 578.5 %all-gather.11.cloned.1.call-start = ((), (), s32[]{:S(2)}) async-start(), calls=%async_computation.14 | async-start | bytes 51904512 | tf_op jit(solution)/shard_map/all_gather | solution.py:46
  9.4 102.4 %copy-start.31 = (f32[2048]{0:T(1024)S(1)}, f32[2048]{0:T(1024)}, u32[]{:S(2)}) copy-start(f32[2048]{0:T(1024)} %param.18) | copy-start | bytes 24580
  9.4 780.2 %all-gather.13.cloned.1.call-start = ((), (), s32[]{:S(2)}) async-start(), calls=%async_computation.15 | async-start | bytes 25952256 | tf_op jit(solution)/shard_map/all_gather | solution.py:46
  10.9 100.9 %copy-start.35 = (f32[256]{0:T(256)}, f32[256]{0:T(256)S(1)}, u32[]{:S(2)}) copy-start(f32[256]{0:T(256)S(1)} %get-tuple-element.328) | copy-start | bytes 3076
  111.8 11.4 copy-start.40
  119.5 8.7 all-to-all-start.1
  123.1 20.2 copy-start.33
  128.1 8.3 all-to-all-start.2
  131.5 11.9 copy-start.38
  136.4 16.8 all-to-all-start
  142.2 16.7 copy-start.16
  165.2 4.4 copy-start.28
  165.2 4.5 copy-start.11
  165.2 4.5 copy-start.18
  169.6 4.7 copy-start.29
  180.9 4.4 copy-start.28
  180.9 4.5 copy-start.11
  180.9 4.5 copy-start.18
  185.3 4.7 copy-start.29
  196.9 17.2 all-to-all-start.3
  214.1 8.1 copy-start.8
  214.1 373.0 %copy-start.21 = (f32[2048]{0:T(1024)S(1)}, f32[2048]{0:T(1024)}, u32[]{:S(2)}) copy-start(f32[2048]{0:T(1024)} %param.21) | copy-start | bytes 24580
  222.3 607.9 %copy-start.24 = (f32[256]{0:T(256)}, f32[256]{0:T(256)S(1)}, u32[]{:S(2)}) copy-start(f32[256]{0:T(256)S(1)} %get-tuple-element.330) | copy-start | bytes 3076
  612.9 195.3 %copy-start.3 = (f32[256,2048]{1,0:T(8,128)S(1)}, f32[256,2048]{1,0:T(8,128)}, u32[]{:S(2)}) copy-start(f32[256,2048]{1,0:T(8,128)} %get-tuple-element.332) | copy-start | bytes 6291460
  832.7 6.5 copy-start.5
  840.3 17.8 all-to-all-start.4
  860.9 134.8 %copy-start.34 = (f32[1,1024]{1,0:T(1,128)S(1)}, f32[1,1024]{1,0:T(1,128)}, u32[]{:S(2)}) copy-start(f32[1,1024]{1,0:T(1,128)} %copy-done.33) | copy-start | bytes 12292
  862.9 3.4 copy-start.30
  888.0 5.8 copy-start
  888.0 5.8 copy-start.9
  888.0 13.4 slice-start
  893.9 7.6 slice-start.1
  901.4 3.7 copy-start.10
  927.6 3.4 copy-start.30
  952.7 5.8 copy-start
  952.7 5.8 copy-start.9
  952.7 13.4 slice-start
  958.6 7.6 slice-start.1
  966.2 3.7 copy-start.10
  990.5 10.6 copy-start.17
  990.5 10.6 copy-start.23
  992.2 10.4 all-to-all-start.7
  1002.7 9.2 all-to-all-start.6
  1006.8 133.5 %reduce-scatter.7.cloned.1.call-start = ((), (), s32[]{:S(2)}) async-start(), calls=%async_computation.16 | async-start | bytes 11796480 | tf_op jit(solution)/shard_map/reduce_scatter | solution.py:61
  1006.9 20.4 copy-start.2
  1006.9 20.4 copy-start.32
  1006.9 20.4 copy-start.36
  1034.1 1.6 copy-start.6
  1034.1 196.4 %reduce-scatter.9.cloned.1.call-start = ((), (), s32[]{:S(2)}) async-start(), calls=%async_computation.17 | async-start | bytes 9437184 | tf_op jit(solution)/shard_map/reduce_scatter | solution.py:61
  1042.7 416.0 %reduce-scatter.11.cloned.1.call-start = ((), (), s32[]{:S(2)}) async-start(), calls=%async_computation.18 | async-start | bytes 25952256 | tf_op jit(solution)/shard_map/reduce_scatter | solution.py:61
  1056.8 1.6 copy-start.4
  1056.8 1.6 copy-start.22
  1056.8 1.6 copy-start.25
  1056.8 846.4 %reduce-scatter.13.cloned.1.call-start = ((), (), s32[]{:S(2)}) async-start(), calls=%async_computation.20 | async-start | bytes 51904512
  1080.2 886.8 %all-gather.15.cloned.1.call-start = ((), (), s32[]{:S(2)}) async-start(), calls=%async_computation.19 | async-start | bytes 6553600 | tf_op jit(solution)/shard_map/all_gather | solution.py:89
  1140.3 1022.9 %all-reduce.5.cloned.1.call-start = ((), (), s32[]{:S(2)}) async-start(), calls=%async_computation.21 | async-start | bytes 19398656 | tf_op jit(solution)/shard_map/psum | solution.py:263
  1903.2 13.2 copy-start.14
  1916.4 8.6 copy-start.37
  1916.4 47.4 %copy-start.7 = (f32[256,2048]{1,0:T(8,128)S(1)}, f32[256,2048]{1,0:T(8,128)}, u32[]{:S(2)}) copy-start(f32[256,2048]{1,0:T(8,128)} %copy-done.5) | copy-start | bytes 6291460
  1916.5 47.4 %copy-start.39 = (f32[256]{0:T(256)S(1)}, f32[256]{0:T(256)}, u32[]{:S(2)}) copy-start(f32[256]{0:T(256)} %get-tuple-element.327) | copy-start | bytes 3076
  2166.0 8.6 copy-start.15
  (7 other events, 6.5 us)
Sparse Core Ops, SparseCore 0:
  9.6 102.0 all-gather.6
  113.3 80.3 all-gather.8
  195.4 391.6 all-gather.10
  588.6 200.9 all-gather.12
  1034.2 106.0 reduce-scatter.6
  1142.5 87.9 reduce-scatter.8
  1232.8 225.7 reduce-scatter.10
  1461.0 442.1 reduce-scatter.12
  1905.0 60.9 all-gather.14
  1969.8 193.3 all-reduce.4
